TPU v7x, 256 devices: a whole 4x4x8 slice. The times are simulated.
256 devices in a mesh: tok: 64 (over z_hi, x, y), head: 4 (over z_lo, core).
Axes of the slice: x: 4, y: 4, z: 8 (z_hi: 4, z_lo: 2; z = z_hi * 2 + z_lo), core: 2. Of those that a mesh axis runs over, the one named last changes fastest.
Arguments:
- queries: bfloat16 [16384, 2560], P('tok', 'head'), may hold values from -140 to 140
- keys: bfloat16 [2048, 2560], P('tok', 'head'), may hold values from -6 to 6
- values: bfloat16 [2048, 2560], P('tok', 'head'), may hold values from -6 to 6
- query_tan: bfloat16 [16384, 2560], P('tok', 'head'), may hold values from -6 to 6
- key_tan: bfloat16 [2048, 2560], P('tok', 'head'), may hold values from -6 to 6
- value_tan: bfloat16 [2048, 2560], P('tok', 'head'), may hold values from -6 to 6
- out_weight: bfloat16 [2560, 5120], P('head'), may hold values from -0.3125 to 0.3125
Outputs:
- output: bfloat16 [16384, 5120], P('tok', 'head')
- output_tan: bfloat16 [16384, 5120], P('tok', 'head')
All inputs are finite; a program needn't handle non-finite values.
Results may differ from a plain program's by a relative error of at most 0.012.
Values may be sent and summed in bfloat16 or wider, within the bound.
No kernel may reach another device: no remote copies, remote signals or barrier semaphores. Data moves between devices by JAX's collectives and lax.ppermute only.
A program may use at most 128 MiB of HBM per device.

v0:
```python
import jax
import jax.numpy as jnp
from jax import lax
from jax.sharding import PartitionSpec as P

HD = 128


def split_rows(array, head_count):
    return array.reshape(array.shape[0], head_count, HD)


def score_pair(query_heads, query_dir_heads, key_piece, key_dir_piece, head_count, score_scale):
    key_heads = split_rows(key_piece, head_count)
    key_dir_heads = split_rows(key_dir_piece, head_count)
    scores = (
        jnp.einsum("thd,rhd->htr", query_heads, key_heads, preferred_element_type=jnp.float32)
        * score_scale
    )
    tangent = (
        jnp.einsum("thd,rhd->htr", query_dir_heads, key_heads, preferred_element_type=jnp.float32)
        + jnp.einsum("thd,rhd->htr", query_heads, key_dir_heads, preferred_element_type=jnp.float32)
    ) * score_scale
    return (scores, tangent)


def apply_weights(weights, value_heads):
    return jnp.einsum("htr,rhd->htd", weights, value_heads, preferred_element_type=jnp.float32)


def join_heads(array, rows_here, head_count):
    return array.transpose(1, 0, 2).reshape(rows_here, head_count * HD).astype(jnp.bfloat16)


def shards(queries, keys, values, query_tan, key_tan, value_tan, out_weight):
    rows_here = queries.shape[0]
    head_count = queries.shape[1] // HD
    score_scale = HD ** (-0.5)
    query_heads = split_rows(queries, head_count)
    query_dir_heads = split_rows(query_tan, head_count)
    lowest = jnp.full((head_count, rows_here), -1e30, jnp.float32)
    stacked_all = jnp.stack((keys, values, key_tan, value_tan))
    stacked_pair = jnp.stack((keys, values))
    pieces = lax.all_gather(stacked_pair, "tok", axis=1, tiled=True)
    key_heads = split_rows(pieces[0], head_count)
    value_heads = split_rows(pieces[1], head_count)
    scores = (
        jnp.einsum("thd,rhd->htr", query_heads, key_heads, preferred_element_type=jnp.float32)
        * score_scale
    )
    peak_new = jnp.maximum(lowest, jnp.max(scores, axis=2))
    exponent = jnp.exp(scores - peak_new[:, :, None])
    row_total = jnp.sum(exponent, axis=2)
    numerator = apply_weights(exponent.astype(jnp.bfloat16), value_heads)
    peak, row_total, numerator = (peak_new, row_total, numerator)
    attended = numerator / row_total[:, :, None]
    pieces = lax.all_gather(stacked_all, "tok", axis=1, tiled=True)
    scores, tangent = score_pair(
        query_heads, query_dir_heads, pieces[0], pieces[2], head_count, score_scale
    )
    value_heads = split_rows(pieces[1], head_count)
    value_dir_heads = split_rows(pieces[3], head_count)
    exponent = jnp.exp(scores - peak[:, :, None])
    weighted = exponent * tangent
    row_total_tan = jnp.sum(weighted, axis=2)
    numerator_tan = apply_weights(weighted.astype(jnp.bfloat16), value_heads) + apply_weights(
        exponent.astype(jnp.bfloat16), value_dir_heads
    )
    row_total_tan, numerator_tan = (row_total_tan, numerator_tan)
    attended_tan = (numerator_tan - attended * row_total_tan[:, :, None]) / row_total[:, :, None]
    partial_value = jnp.dot(
        join_heads(attended, rows_here, head_count), out_weight, preferred_element_type=jnp.float32
    )
    partial_tan = jnp.dot(
        join_heads(attended_tan, rows_here, head_count),
        out_weight,
        preferred_element_type=jnp.float32,
    )
    output, output_tan = (
        lax.psum_scatter(
            partial_value.astype(jnp.bfloat16), "head", scatter_dimension=1, tiled=True
        ).astype(jnp.float32),
        lax.psum_scatter(
            partial_tan.astype(jnp.bfloat16), "head", scatter_dimension=1, tiled=True
        ).astype(jnp.float32),
    )
    return (output.astype(jnp.bfloat16), output_tan.astype(jnp.bfloat16))


def solution(mesh):
    in_specs = (
        P("tok", "head"),
        P("tok", "head"),
        P("tok", "head"),
        P("tok", "head"),
        P("tok", "head"),
        P("tok", "head"),
        P("head", None),
    )
    out_specs = (P("tok", "head"), P("tok", "head"))
    return jax.shard_map(shards, mesh=mesh, in_specs=in_specs, out_specs=out_specs, check_vma=False)
```

profile of v0, /device:TPU:1, one launch (start us, length us, event | category | flops | bytes accessed | tf_op | source)
XLA Modules:
  0.0 385.8 jit_solution(15764494412756072858)
XLA Ops:
  7.2 0.8 pad_maximum_fusion.1
  8.0 0.7 copy.34
  8.7 0.0 all-gather.5.cloned.1.call-start
  8.8 0.9 pad_maximum_fusion
  9.7 0.8 copy.41
  10.5 0.0 reduce-scatter.3.cloned.1.call-start
  10.5 1.1 copy.36
  11.6 1.1 copy.45
  12.8 97.5 %all-gather.3.cloned.1.call-done = bf16[2,2048,640]{2,0,1:T(2,128)(2,1)} async-done(((bf16[2,32,640]{2,0,1:T(2,128)(2,1)}), bf16[2,2048,640]{2,0,1:T(2,128)(2,1)}) %all-gather.3.cloned.1.call-update) | async-done | bytes 5242896 | tf_op jit(solution)/shard_map/all_gather | solution.py:44
  110.3 11.9 %fusion.38 = (bf16[1,2048,640]{2,0,1:T(2,128)(2,1)}, bf16[1,2048,640]{2,0,1:T(2,128)(2,1)}) fusion(bf16[2,2048,640]{2,0,1:T(2,128)(2,1)} %all-gather.3.cloned.1.call-done), kind=kLoop, calls=%fused_computation.32 | loop fusion | bytes 10485760 | tf_op jit(solution)/shard_map/slice | solution.py:45
  122.2 9.7 %copy.64 = bf16[1,2048,640]{1,2,0:T(8,128)(2,1)S(1)} copy(bf16[1,2048,640]{2,0,1:T(2,128)(2,1)} %get-tuple-element.6) | data formatting | bytes 5242880
  131.9 11.1 %copy.39 = bf16[1,2048,640]{1,2,0:T(8,128)(2,1)} copy(bf16[1,2048,640]{2,0,1:T(2,128)(2,1)} %get-tuple-element.7) | data formatting | bytes 5242880 | tf_op jit(solution)/shard_map/slice | solution.py:46
  143.0 1.6 bitcast_reduce_fusion.1
  144.7 1.7 fusion.2
  146.4 2.7 fusion.39
  149.1 3.7 convolution_convert_fusion.1
  152.9 0.2 reduce-scatter.5.cloned.1.call-start
  153.1 86.9 %all-gather.5.cloned.1.call-done = bf16[4,2048,640]{2,0,1:T(4,128)(2,1)} async-done(((bf16[4,32,640]{2,0,1:T(4,128)(2,1)}), bf16[4,2048,640]{2,0,1:T(4,128)(2,1)}) %all-gather.5.cloned.1.call-update) | async-done | bytes 10485776 | tf_op jit(solution)/shard_map/all_gather | solution.py:57
  240.0 28.6 %fusion.37 = (bf16[1,2048,640]{2,0,1:T(2,128)(2,1)}, bf16[1,2048,640]{2,0,1:T(2,128)(2,1)}, bf16[1,2048,640]{2,0,1:T(2,128)(2,1)}, bf16[1,2048,640]{2,0,1:T(2,128)(2,1)}) fusion(bf16[4,2048,640]{2,0,1:T(4,128)(2,1)} %all-gather.5.cloned.1.call-done), kind=kLoop, calls=%fused_computation.31 | loop fusion | bytes 20971520 | tf_op jit(solution)/shard_map/slice | solution.py:62
  268.6 11.1 %copy.53 = bf16[1,2048,640]{1,2,0:T(8,128)(2,1)} copy(bf16[1,2048,640]{2,0,1:T(2,128)(2,1)} %get-tuple-element.2) | data formatting | bytes 5242880 | tf_op jit(solution)/shard_map/slice | solution.py:62
  279.7 9.7 %copy.65 = bf16[1,2048,640]{1,2,0:T(8,128)(2,1)S(1)} copy(bf16[1,2048,640]{2,0,1:T(2,128)(2,1)} %get-tuple-element.3) | data formatting | bytes 5242880
  289.4 11.1 %copy.51 = bf16[1,2048,640]{1,2,0:T(8,128)(2,1)} copy(bf16[1,2048,640]{2,0,1:T(2,128)(2,1)} %get-tuple-element.4) | data formatting | bytes 5242880 | tf_op jit(solution)/shard_map/slice | solution.py:61
  300.5 11.1 %copy.66 = bf16[1,2048,640]{1,2,0:T(8,128)(2,1)} copy(bf16[1,2048,640]{2,0,1:T(2,128)(2,1)} %get-tuple-element.5) | data formatting | bytes 5242880
  311.6 5.5 %fusion.42 = f32[5,2048,256]{2,1,0:T(8,128)} fusion(bf16[2048,5,128]{0,2,1:T(8,128)(2,1)S(1)} %bitcast.70, bf16[256,5,128]{0,2,1:T(8,128)(2,1)S(1)} %bitcast.76), kind=kOutput, calls=%fused_computation.36 | convolution fusion | flops 671088640 | bytes 13434880 | tf_op jit(solution)/shard_map/thd,rhd->htr/dot_general | solution.py:17
  317.2 5.5 %fusion.43 = f32[5,2048,256]{2,1,0:T(8,128)} fusion(bf16[2048,5,128]{0,2,1:T(8,128)(2,1)S(1)} %bitcast.71, bf16[256,5,128]{0,2,1:T(8,128)(2,1)S(1)} %bitcast.80), kind=kOutput, calls=%fused_computation.37 | convolution fusion | flops 671088640 | bytes 13434880 | tf_op jit(solution)/shard_map/thd,rhd->htr/dot_general | solution.py:21
  322.7 10.3 %bitcast_reduce_fusion = (f32[5,256]{1,0:T(8,128)S(1)}, bf16[5,2048,256]{2,1,0:T(8,128)(2,1)S(1)}) fusion(f32[5,2048,256]{2,1,0:T(8,128)} %fusion.43, bf16[2048,5,128]{0,2,1:T(8,128)(2,1)} %bitcast.73, bf16[256,5,128]{0,2,1:T(8,128)(2,1)S(1)} %bitcast.77, f32[5,256]{1,0:T(8,128)S(1)} %broadcast_maximum_fusion, f32[5,2048,256]{2,1,0:T(8,128)} %fusion.42), kind=kOutput, calls=%fused_computation | convolution fusion | flops 689437440 | bytes 29173760 | tf_op jit(solution)/shard_map/thd,rhd->htr/dot_general | solution.py:22
  333.0 0.8 fusion.40
  333.9 0.8 copy-done.1
  334.7 0.1 copy-done.3
  334.8 6.3 %fusion.31 = bf16[256,5,128]{0,2,1:T(8,128)(2,1)S(1)} fusion(f32[5,256,128]{1,2,0:T(8,128)S(1)} %fusion.40, bf16[2048,5,128]{0,2,1:T(8,128)(2,1)S(1)} %bitcast.78, f32[5,2048,256]{2,1,0:T(8,128)} %fusion.42, f32[5,256]{1,0:T(8,128)S(1)} %broadcast_maximum_fusion, f32[256,5,128]{0,2,1:T(8,128)S(1)} %copy-done.3, f32[256,5]{0,1:T(8,128)S(1)} %bitcast.91, ...), kind=kOutput, calls=%fused_computation.25 | convolution fusion | flops 679772160 | bytes 14760960 | tf_op jit(solution)/shard_map/htr,rhd->htd/dot_general | solution.py:28
  341.2 3.8 convolution_convert_fusion
  345.1 34.2 %reduce-scatter.5.cloned.1.call-done = bf16[256,1280]{1,0:T(8,128)(2,1)} async-done(((bf16[256,5120]{1,0:T(8,128)(2,1)}), bf16[256,1280]{1,0:T(8,128)(2,1)}) %reduce-scatter.5.cloned.1.call-update) | async-done | bytes 655376 | tf_op jit(solution)/shard_map/reduce_scatter | solution.py:83
  (23 shorter events, 0.2 us)
Async XLA Ops:
  7.2 103.1 %all-gather.3.cloned.1.call-start = ((), (), s32[]{:S(2)}) async-start(), calls=%async_computation.2 | async-start | bytes 5324800 | tf_op jit(solution)/shard_map/all_gather | solution.py:44
  8.7 231.3 %all-gather.5.cloned.1.call-start = ((), (), s32[]{:S(2)}) async-start(), calls=%async_computation.4 | async-start | bytes 10649600 | tf_op jit(solution)/shard_map/all_gather | solution.py:57
  10.5 334.6 %reduce-scatter.3.cloned.1.call-start = ((), (), s32[]{:S(2)}) async-start(), calls=%async_computation.3 | async-start | bytes 3276800 | tf_op jit(solution)/shard_map/reduce_scatter | solution.py:80
  144.6 1.7 copy-start.2
  144.6 4.5 %slice-start = ((s8[6553600]{0:T(1024)(128)(4,1)}), s8[4194304]{0:T(1024)(128)(4,1)S(1)}, s32[]{:S(2)}) async-start(s8[6553600]{0:T(1024)(128)(4,1)} %bitcast.66), calls=%async_computation.6 | async-start | bytes 8388608
  146.4 2.8 slice-start.1
  152.9 226.3 %reduce-scatter.5.cloned.1.call-start = ((), (), s32[]{:S(2)}) async-start(), calls=%async_computation.5 | async-start | bytes 3276800 | tf_op jit(solution)/shard_map/reduce_scatter | solution.py:83
  322.7 10.3 %copy-start = (bf16[1,2048,640]{1,2,0:T(8,128)(2,1)S(1)}, bf16[1,2048,640]{1,2,0:T(8,128)(2,1)}, u32[]{:S(2)}) copy-start(bf16[1,2048,640]{1,2,0:T(8,128)(2,1)} %copy.51) | copy-start | bytes 7864324
  333.0 1.7 copy-start.1
  333.0 1.9 copy-start.3
  333.0 8.2 %slice-start.2 = ((s8[6553600]{0:T(1024)(128)(4,1)}), s8[4194304]{0:T(1024)(128)(4,1)S(1)}, s32[]{:S(2)}) async-start(s8[6553600]{0:T(1024)(128)(4,1)} %bitcast.68), calls=%async_computation.8 | async-start | bytes 8388608
  334.8 6.3 %slice-start.3 = ((s8[6553600]{0:T(1024)(128)(4,1)}), s8[2359296]{0:T(1024)(128)(4,1)S(1)}, s32[]{:S(2)}) async-start(s8[6553600]{0:T(1024)(128)(4,1)} %bitcast.68), calls=%async_computation.9 | async-start | bytes 4718592
Sparse Core Ops, SparseCore 0:
  11.8 98.3 all-gather.2
  113.6 126.3 all-gather.4
  243.1 33.9 reduce-scatter.2
  345.2 34.0 reduce-scatter.4
where the time goes:
time: 387 us; the launch traced here: 386 us
  waiting for transfers between devices  219 us (57%)
  local copies, waits for them, and re-layouts  109 us (28%)
  matrix products  40.4 us (10%)
  between operations  13.9 us (4%)
    all_gather x1, waiting for transfers between devices, shards(): pieces = lax.all_gather(stacked_pair, 'tok', axis=1, tiled=True)  97.5 us
    all_gather x1, waiting for transfers between devices, shards(): pieces = lax.all_gather(stacked_all, 'tok', axis=1, tiled=True)  86.9 us
    slice x2, local copies, waits for them, and re-layouts, shards(): value_dir_heads = split_rows(pieces[3], head_count)  39.7 us
    reduce_scatter x1, waiting for transfers between devices, shards(): lax.psum_scatter(partial_tan.astype(jnp.bfloat16), 'head', scatter_dimens...  34.2 us
    unnamed x21, local copies, waits for them, and re-layouts  33.8 us
    slice x2, local copies, waits for them, and re-layouts, shards(): value_heads = split_rows(pieces[1], head_count)  22.3 us
    slice x1, local copies, waits for them, and re-layouts, shards(): key_heads = split_rows(pieces[0], head_count)  11.9 us
    dot_general x1, matrix products, score_pair(): jnp.einsum('thd,rhd->htr', query_heads, key_dir_heads, preferred_element_...  10.3 us
  transfers between devices with their start and end apart: 4, of which 3 were waited for; matrix products, arithmetic and copies ran while one was open for 39% of the time, Pallas kernels for 0%

commit v1 on v0

--- a/solution.py
+++ b/solution.py
@@ -54,7 +54,7 @@
     numerator = apply_weights(exponent.astype(jnp.bfloat16), value_heads)
     peak, row_total, numerator = (peak_new, row_total, numerator)
     attended = numerator / row_total[:, :, None]
-    pieces = lax.all_gather(stacked_all, "tok", axis=1, tiled=True)
+    pieces = jnp.concatenate(lax.all_gather(stacked_all, "tok"), axis=1)
     scores, tangent = score_pair(
         query_heads, query_dir_heads, pieces[0], pieces[2], head_count, score_scale
     )

time: 387 us -> 353 us (0.912)
  local copies, waits for them, and re-layouts: 109 us -> 76.3 us
    slice x2 -> x1, local copies, waits for them, and re-layouts: 39.7 us -> 7.31 us  [shards(): value_dir_heads = split_rows(pieces[3], head_count)]
    another operation x1 -> x4, local copies, waits for them, and re-layouts: 0.76 us -> 25.2 us  [split_rows(): return array.reshape(array.shape[0], head_count, HD)]
    unnamed x21 -> x23, local copies, waits for them, and re-layouts: 33.8 us -> 11.1 us
    slice x2 -> x1, local copies, waits for them, and re-layouts: 22.3 us -> 11.1 us  [shards(): value_heads = split_rows(pieces[1], head_count)]
    all_gather x0 -> x1, local copies, waits for them, and re-layouts: none -> 9.02 us  [shards(): pieces = jnp.concatenate(lax.all_gather(stacked_all, 'tok'), axis=1)]
  transfers between devices with their start and end apart: 4 -> 4, of which waited for: 3 -> 3; matrix products, arithmetic and copies ran while one was open for 39% -> 33% of each run, Pallas kernels for 0% -> 0%
where the time goes in v1:
time: 353 us; the launch traced here: 352 us
  waiting for transfers between devices  220 us (62%)
  local copies, waits for them, and re-layouts  76.3 us (22%)
  matrix products  37.9 us (11%)
  between operations  13.9 us (4%)
  other arithmetic  4.07 us (1%)
    all_gather x1, waiting for transfers between devices, shards(): pieces = lax.all_gather(stacked_pair, 'tok', axis=1, tiled=True)  98.7 us
    all_gather x1, waiting for transfers between devices, shards(): pieces = jnp.concatenate(lax.all_gather(stacked_all, 'tok'), axis=1)  86.7 us
    reduce_scatter x1, waiting for transfers between devices, shards(): lax.psum_scatter(partial_tan.astype(jnp.bfloat16), 'head', scatter_dimens...  34.1 us
    another operation x4, local copies, waits for them, and re-layouts, split_rows(): return array.reshape(array.shape[0], head_count, HD)  25.2 us
    slice x1, local copies, waits for them, and re-layouts, shards(): key_heads = split_rows(pieces[0], head_count)  11.8 us
    dot_general x3, matrix products, apply_weights(): jnp.einsum('htr,rhd->htd', weights, value_heads, preferred_element_type=j...  11.2 us
    slice x1, local copies, waits for them, and re-layouts, shards(): value_heads = split_rows(pieces[1], head_count)  11.1 us
    unnamed x23, local copies, waits for them, and re-layouts  11.1 us
  transfers between devices with their start and end apart: 4, of which 3 were waited for; matrix products, arithmetic and copies ran while one was open for 33% of the time, Pallas kernels for 0%

profile of v1, /device:TPU:1, one launch (start us, length us, event | category | flops | bytes accessed | tf_op | source)
XLA Modules:
  0.0 352.1 jit_solution(7211859784138011922)
XLA Ops:
  7.2 0.0 all-gather.4.cloned.1.call-start
  7.2 0.8 pad_maximum_fusion.1
  8.0 0.7 copy.36
  8.7 0.0 all-gather.6.cloned.1.call-start
  8.8 1.5 pad_maximum_fusion
  10.4 0.0 reduce-scatter.3.cloned.1.call-start
  10.4 1.1 copy.38
  11.6 98.7 %all-gather.4.cloned.1.call-done = bf16[2,2048,640]{2,0,1:T(2,128)(2,1)} async-done(((bf16[2,32,640]{2,0,1:T(2,128)(2,1)}), bf16[2,2048,640]{2,0,1:T(2,128)(2,1)}) %all-gather.4.cloned.1.call-update) | async-done | bytes 5242896 | tf_op jit(solution)/shard_map/all_gather | solution.py:44
  110.3 11.8 %fusion.55 = (bf16[1,2048,640]{2,0,1:T(2,128)(2,1)}, bf16[1,2048,640]{2,0,1:T(2,128)(2,1)}) fusion(bf16[2,2048,640]{2,0,1:T(2,128)(2,1)} %all-gather.4.cloned.1.call-done), kind=kLoop, calls=%fused_computation.40 | loop fusion | bytes 10485760 | tf_op jit(solution)/shard_map/slice | solution.py:45
  122.1 9.7 %copy.61 = bf16[1,2048,640]{1,2,0:T(8,128)(2,1)S(1)} copy(bf16[1,2048,640]{2,0,1:T(2,128)(2,1)} %get-tuple-element.6) | data formatting | bytes 5242880
  131.8 11.1 %copy.41 = bf16[1,2048,640]{1,2,0:T(8,128)(2,1)} copy(bf16[1,2048,640]{2,0,1:T(2,128)(2,1)} %get-tuple-element.7) | data formatting | bytes 5242880 | tf_op jit(solution)/shard_map/slice | solution.py:46
  142.9 1.6 bitcast_reduce_fusion.1
  144.5 1.7 fusion.2
  146.3 2.7 fusion.56
  149.0 3.8 %convolution_convert_fusion.1 = bf16[256,5120]{1,0:T(8,128)(2,1)} fusion(bf16[256,640]{0,1:T(8,128)(2,1)S(1)} %bitcast.82, bf16[640,5120]{1,0:T(8,128)(2,1)S(1)} %bitcast.71), kind=kOutput, calls=%fused_computation.12 | convolution fusion | flops 1679032320 | bytes 9502720 | tf_op jit(solution)/shard_map/dot_general | solution.py:71
  152.8 0.2 reduce-scatter.5.cloned.1.call-start
  153.1 0.2 copy.46
  153.2 86.7 %all-gather.6.cloned.1.call-done = bf16[256,32,640]{2,1,0:T(8,128)(2,1)} async-done(((bf16[4,32,640]{2,1,0:T(8,128)(2,1)}), bf16[256,32,640]{2,1,0:T(8,128)(2,1)}) %all-gather.6.cloned.1.call-update) | async-done | bytes 10485776 | tf_op jit(solution)/shard_map/all_gather | solution.py:57
  240.0 9.0 %copy.85 = bf16[64,4,32,640]{3,2,0,1:T(8,128)(2,1)} copy(bf16[64,4,32,640]{3,2,1,0:T(8,128)(2,1)} %bitcast.74) | data formatting | bytes 20971520 | tf_op jit(solution)/shard_map/all_gather | solution.py:57
  249.0 7.3 %fusion.54 = (bf16[1,64,32,640]{3,2,1,0:T(8,128)(2,1)S(1)}, bf16[1,64,32,640]{3,2,1,0:T(8,128)(2,1)}, bf16[1,64,32,640]{3,2,1,0:T(8,128)(2,1)}, bf16[1,64,32,640]{3,2,1,0:T(8,128)(2,1)}) fusion(bf16[4,64,32,640]{3,2,1,0:T(8,128)(2,1)} %bitcast.69), kind=kLoop, calls=%fused_computation.39 | loop fusion | bytes 20971520 | tf_op jit(solution)/shard_map/slice | solution.py:62
  256.3 7.0 %reshape_squeeze.22 = bf16[2048,5,128]{2,1,0:T(8,128)(2,1)} reshape(bf16[1,64,32,640]{3,2,1,0:T(8,128)(2,1)} %get-tuple-element.3) | data formatting | bytes 5242880 | tf_op jit(solution)/shard_map/reshape;squeeze | solution.py:10
  263.3 7.0 %reshape_squeeze.20 = bf16[2048,5,128]{2,1,0:T(8,128)(2,1)} reshape(bf16[1,64,32,640]{3,2,1,0:T(8,128)(2,1)} %get-tuple-element.5) | data formatting | bytes 5242880 | tf_op jit(solution)/shard_map/reshape;squeeze | solution.py:10
  270.3 7.0 %reshape_squeeze.21 = bf16[2048,5,128]{2,1,0:T(8,128)(2,1)} reshape(bf16[1,64,32,640]{3,2,1,0:T(8,128)(2,1)} %get-tuple-element.4) | data formatting | bytes 5242880 | tf_op jit(solution)/shard_map/reshape;squeeze | solution.py:10
  277.4 4.2 %reshape_squeeze.23 = bf16[2048,5,128]{2,1,0:T(8,128)(2,1)} reshape(bf16[1,64,32,640]{3,2,1,0:T(8,128)(2,1)S(1)} %get-tuple-element.2) | data formatting | bytes 5242880 | tf_op jit(solution)/shard_map/reshape;squeeze | solution.py:10
  281.6 3.9 %fusion.18 = f32[5,2048,256]{2,1,0:T(8,128)S(1)} fusion(bf16[256,5,128]{0,2,1:T(8,128)(2,1)S(1)} %bitcast.77, bf16[2048,5,128]{2,1,0:T(8,128)(2,1)} %reshape_squeeze.20), kind=kOutput, calls=%fused_computation.25 | convolution fusion | flops 671088640 | bytes 13434880 | tf_op jit(solution)/shard_map/thd,rhd->htr/dot_general | solution.py:17
  285.4 5.5 %fusion.16 = f32[5,2048,256]{2,1,0:T(8,128)} fusion(bf16[256,5,128]{0,2,1:T(8,128)(2,1)S(1)} %bitcast.80, bf16[2048,5,128]{2,1,0:T(8,128)(2,1)S(1)} %copy-done), kind=kOutput, calls=%fused_computation.23 | convolution fusion | flops 671088640 | bytes 13434880 | tf_op jit(solution)/shard_map/thd,rhd->htr/dot_general | solution.py:21
  290.9 8.2 %bitcast_reduce_fusion = (f32[5,256]{1,0:T(8,128)S(1)}, bf16[5,2048,256]{2,1,0:T(8,128)(2,1)}) fusion(f32[5,2048,256]{2,1,0:T(8,128)} %fusion.16, bf16[256,5,128]{0,2,1:T(8,128)(2,1)S(1)} %bitcast.78, bf16[2048,5,128]{2,1,0:T(8,128)(2,1)S(1)} %copy-done.2, f32[5,256]{1,0:T(8,128)S(1)} %broadcast_maximum_fusion, f32[5,2048,256]{2,1,0:T(8,128)S(1)} %fusion.18), kind=kOutput, calls=%fused_computation | convolution fusion | flops 689437440 | bytes 29173760 | tf_op jit(solution)/shard_map/thd,rhd->htr/dot_general | solution.py:22
  299.2 4.7 %fusion.8 = f32[5,256,128]{1,2,0:T(8,128)} fusion(bf16[2048,5,128]{2,1,0:T(8,128)(2,1)S(1)} %copy-done.1, bf16[5,2048,256]{2,1,0:T(8,128)(2,1)} %get-tuple-element.13), kind=kOutput, calls=%fused_computation.15 | convolution fusion | flops 671088640 | bytes 8519680 | tf_op jit(solution)/shard_map/htr,rhd->htd/dot_general | solution.py:28
  303.9 3.7 %fusion.46 = bf16[256,5,128]{0,2,1:T(8,128)(2,1)S(1)} fusion(f32[5,256,128]{1,2,0:T(8,128)} %fusion.8, f32[5,2048,256]{2,1,0:T(8,128)S(1)} %fusion.18, f32[5,256]{1,0:T(8,128)S(1)} %broadcast_maximum_fusion, bf16[2048,5,128]{2,1,0:T(8,128)(2,1)S(1)} %copy-done.3, f32[256,5,128]{0,2,1:T(8,128)} %get-tuple-element.11, f32[256,5]{0,1:T(8,128)S(1)} %bitcast.91, ...), kind=kOutput, calls=%fused_computation.33 | convolution fusion | flops 679772160 | bytes 14760960 | tf_op jit(solution)/shard_map/htr,rhd->htd/dot_general | solution.py:28
  307.6 3.8 %convolution_convert_fusion = bf16[256,5120]{1,0:T(8,128)(2,1)} fusion(bf16[256,640]{0,1:T(8,128)(2,1)S(1)} %bitcast.81, bf16[640,5120]{1,0:T(8,128)(2,1)S(1)} %bitcast.73), kind=kOutput, calls=%fused_computation.11 | convolution fusion | flops 1679032320 | bytes 9502720 | tf_op jit(solution)/shard_map/dot_general | solution.py:74
  311.4 0.0 reduce-scatter.3.cloned.1.call-done
  311.5 34.1 %reduce-scatter.5.cloned.1.call-done = bf16[256,1280]{1,0:T(8,128)(2,1)} async-done(((bf16[256,5120]{1,0:T(8,128)(2,1)}), bf16[256,1280]{1,0:T(8,128)(2,1)}) %reduce-scatter.5.cloned.1.call-update) | async-done | bytes 655376 | tf_op jit(solution)/shard_map/reduce_scatter | solution.py:83
  (27 shorter events, 0.1 us)
Async XLA Ops:
  7.2 103.1 %all-gather.4.cloned.1.call-start = ((), (), s32[]{:S(2)}) async-start(), calls=%async_computation.2 | async-start | bytes 5324800 | tf_op jit(solution)/shard_map/all_gather | solution.py:44
  8.7 231.2 %all-gather.6.cloned.1.call-start = ((), (), s32[]{:S(2)}) async-start(), calls=%async_computation.5 | async-start | bytes 10649600 | tf_op jit(solution)/shard_map/all_gather | solution.py:57
  10.4 301.1 %reduce-scatter.3.cloned.1.call-start = ((), (), s32[]{:S(2)}) async-start(), calls=%async_computation.3 | async-start | bytes 3276800 | tf_op jit(solution)/shard_map/reduce_scatter | solution.py:80
  144.5 1.7 copy-start.4
  144.5 4.5 %slice-start = ((s8[6553600]{0:T(1024)(128)(4,1)}), s8[4194304]{0:T(1024)(128)(4,1)S(1)}, s32[]{:S(2)}) async-start(s8[6553600]{0:T(1024)(128)(4,1)} %bitcast.70), calls=%async_computation.6 | async-start | bytes 8388608
  146.2 2.8 slice-start.1
  149.0 4.0 %copy-start.5 = (bf16[256,640]{1,0:T(8,128)(2,1)S(1)}, bf16[256,640]{1,0:T(8,128)(2,1)}, u32[]{:S(2)}) copy-start(bf16[256,640]{1,0:T(8,128)(2,1)} %param.10) | copy-start | bytes 983044
  152.8 192.7 %reduce-scatter.5.cloned.1.call-start = ((), (), s32[]{:S(2)}) async-start(), calls=%async_computation.4 | async-start | bytes 3276800 | tf_op jit(solution)/shard_map/reduce_scatter | solution.py:83
  281.6 3.9 %copy-start = (bf16[2048,5,128]{2,1,0:T(8,128)(2,1)S(1)}, bf16[2048,5,128]{2,1,0:T(8,128)(2,1)}, u32[]{:S(2)}) copy-start(bf16[2048,5,128]{2,1,0:T(8,128)(2,1)} %reshape_squeeze.20) | copy-start | bytes 7864324
  285.4 5.5 %copy-start.2 = (bf16[2048,5,128]{2,1,0:T(8,128)(2,1)S(1)}, bf16[2048,5,128]{2,1,0:T(8,128)(2,1)}, u32[]{:S(2)}) copy-start(bf16[2048,5,128]{2,1,0:T(8,128)(2,1)} %reshape_squeeze.21) | copy-start | bytes 7864324
  290.9 8.2 %copy-start.1 = (bf16[2048,5,128]{2,1,0:T(8,128)(2,1)S(1)}, bf16[2048,5,128]{2,1,0:T(8,128)(2,1)}, u32[]{:S(2)}) copy-start(bf16[2048,5,128]{2,1,0:T(8,128)(2,1)} %reshape_squeeze.22) | copy-start | bytes 7864324
  299.1 4.7 %copy-start.3 = (bf16[2048,5,128]{2,1,0:T(8,128)(2,1)S(1)}, bf16[2048,5,128]{2,1,0:T(8,128)(2,1)}, u32[]{:S(2)}) copy-start(bf16[2048,5,128]{2,1,0:T(8,128)(2,1)} %reshape_squeeze.23) | copy-start | bytes 7864324
  299.1 8.4 %slice-start.2 = ((s8[6553600]{0:T(1024)(128)(4,1)}), s8[4194304]{0:T(1024)(128)(4,1)S(1)}, s32[]{:S(2)}) async-start(s8[6553600]{0:T(1024)(128)(4,1)} %bitcast.72), calls=%async_computation.8 | async-start | bytes 8388608
  303.9 3.7 %slice-start.3 = ((s8[6553600]{0:T(1024)(128)(4,1)}), s8[2359296]{0:T(1024)(128)(4,1)S(1)}, s32[]{:S(2)}) async-start(s8[6553600]{0:T(1024)(128)(4,1)} %bitcast.72), calls=%async_computation.9 | async-start | bytes 4718592
Sparse Core Ops, SparseCore 0:
  11.8 98.3 all-gather.3
  113.6 126.3 all-gather.5
  243.1 33.9 reduce-scatter.2
  311.6 33.9 reduce-scatter.4
